TPU v7x, 256 devices: a whole 4x4x8 slice. The times are simulated.
256 devices in a mesh: dp: 4 (over x), pipe: 4 (over z_hi, core), tensor: 16 (over y, z_lo).
Axes of the slice: x: 4, y: 4, z: 8 (z_hi: 2, z_lo: 4; z = z_hi * 4 + z_lo), core: 2. Of those that a mesh axis runs over, the one named last changes fastest.
Arguments:
- inputs: bfloat16 [4, 896, 8192], P('pipe', 'dp', 'tensor'), may hold values from -6 to 6
- cotangent: bfloat16 [896, 8192], P('dp', 'tensor'), may hold values from -6 to 6
- up_first: bfloat16 [4, 32, 256, 256], P('pipe', 'tensor'), may hold values from -0.375 to 0.375
- up_second: bfloat16 [4, 32, 256, 1024], P('pipe', 'tensor'), may hold values from -0.375 to 0.375
- down_first: bfloat16 [4, 32, 1024, 256], P('pipe', 'tensor'), may hold values from -0.1875 to 0.1875
- down_second: bfloat16 [4, 32, 256, 256], P('pipe', 'tensor'), may hold values from -0.375 to 0.375
Outputs:
- grad_inputs: bfloat16 [4, 896, 8192], P('pipe', 'dp', 'tensor')
- grad_up_first: float32 [4, 32, 256, 256], P('pipe', 'tensor', 'dp')
- grad_up_second: float32 [4, 32, 256, 1024], P('pipe', 'tensor', 'dp')
- grad_down_first: float32 [4, 32, 1024, 256], P('pipe', 'tensor', 'dp')
- grad_down_second: float32 [4, 32, 256, 256], P('pipe', 'tensor', 'dp')
All inputs are finite; a program needn't handle non-finite values.
Results may differ from a plain program's by a relative error of at most 0.018.
Values may be sent and summed in bfloat16 or wider, within the bound.
No kernel may reach another device: no remote copies, remote signals or barrier semaphores. Data moves between devices by JAX's collectives and lax.ppermute only.
A program may use at most 64 MiB of HBM per device.

v0:
```python
import functools
import math

import jax
import jax.numpy as jnp
from jax import lax
from jax.experimental import pallas as pl
from jax.experimental.pallas import tpu as pltpu
from jax.sharding import PartitionSpec as P


root_half = 1.0 / math.sqrt(2.0)
norm_density = 1.0 / math.sqrt(2.0 * math.pi)
f32 = jnp.float32
bf16 = jnp.bfloat16


def dot(a, b, dims):
    return lax.dot_general(a, b, (dims, ((), ())), preferred_element_type=f32)


def nn(a, b):
    return dot(a, b, ((1,), (0,)))


def nt(a, b):
    return dot(a, b, ((1,), (1,)))


def tn(a, b):
    return dot(a, b, ((0,), (0,)))


def pack(out_ref, at, parts, tokens):
    lanes = parts[0].shape[1] // 2
    extra = tokens - lanes
    peers = out_ref.shape[0]
    groups = []
    shaped = [part.reshape(peers, 2, 8, 2 * lanes) for part in parts]
    for block in range(2):
        for local in range(2):
            groups.append(shaped[local][:, block])
    lane = lax.broadcasted_iota(jnp.int32, (peers * 8, lanes), 1)
    last = groups[3][..., lanes:].reshape(peers * 8, lanes)
    for n, group in enumerate(groups):
        out_ref[:, at + n] = group[..., :lanes].astype(bf16)
        if n < 3:
            rest = group[..., lanes:].reshape(peers * 8, lanes)
            moved = pltpu.roll(last, extra - n * (lanes - extra), 1)
            joined = jnp.where(lane < extra, rest, moved)
            out_ref[:, at + 4 + n] = joined.reshape(peers, 8, lanes).astype(bf16)


def unpack(ref, at, block, tokens):
    peers, _, _, lanes = ref.shape
    extra = tokens - lanes
    lane = lax.broadcasted_iota(jnp.int32, (peers * 8, lanes), 1)

    def group(n):
        return ref[:, at + n].astype(f32)

    parts = []
    for n in (2 * block, 2 * block + 1):
        if n < 3:
            rest = jnp.where(lane < extra, group(4 + n).reshape(peers * 8, lanes), 0.0)
        else:
            rest = jnp.zeros((peers * 8, lanes), f32)
            for m in range(3):
                low = m * (lanes - extra)
                piece = pltpu.roll(
                    group(4 + m).reshape(peers * 8, lanes), (low + lanes - extra) % lanes, 1
                )
                inside = (lane >= low) & (lane < low + lanes - extra)
                rest = jnp.where(inside, piece, rest)
        parts.append(jnp.concatenate([group(n), rest.reshape(peers, 8, lanes)], axis=2))
    joined = jnp.stack(parts, axis=1)
    return joined.reshape(peers * 16, 2 * lanes).astype(bf16)


def near(value):
    return pltpu.with_memory_space_constraint(value, pltpu.VMEM)


def held(value):
    return pltpu.VMEM(value.shape, value.dtype)


def call(body, outs, args, flops=0, scalars=0, scratch=(), room=12):
    moved = sum(a.size * a.dtype.itemsize for a in args) + sum(
        math.prod(o.shape) * o.dtype.itemsize for o in outs
    )
    specs = [pl.BlockSpec(memory_space=pltpu.SMEM)] * scalars
    specs += [pl.BlockSpec(memory_space=pltpu.VMEM)] * (len(args) - scalars)
    return pl.pallas_call(
        body,
        out_shape=outs,
        scratch_shapes=scratch,
        in_specs=specs,
        out_specs=[pl.BlockSpec(memory_space=pltpu.VMEM)] * len(outs),
        compiler_params=pltpu.CompilerParams(vmem_limit_bytes=room * 2**20),
        cost_estimate=pl.CostEstimate(flops=flops, bytes_accessed=moved, transcendentals=0),
    )(*args)


def struct(shape, dtype=bf16):
    return jax.ShapeDtypeStruct(shape, dtype)


def padded(value, rows):
    zeros = jnp.zeros((rows - value.shape[0], value.shape[1]), value.dtype)
    return jnp.concatenate([value, zeros], axis=0)


def stage_kernel(*refs):
    half = len(refs) // 2
    for source, target in zip(refs[:half], refs[half:]):
        target[...] = source[...]


def first_parts(x_ref, u1_ref, lanes):
    width = u1_ref.shape[1]
    parts = []
    for i in range(2):
        cols = slice(i * width, (i + 1) * width)
        parts.append(nn(padded(x_ref[:, cols], lanes), u1_ref[i]).T)
    return parts


def last_parts(g_ref, d2_ref, lanes):
    width = d2_ref.shape[1]
    parts = []
    for i in range(2):
        cols = slice(i * width, (i + 1) * width)
        parts.append(nt(d2_ref[i], padded(g_ref[:, cols], lanes)))
    return parts


def entry_kernel(x_ref, u1_ref, out_ref):
    pack(out_ref, 0, first_parts(x_ref, u1_ref, 2 * out_ref.shape[3]), x_ref.shape[0])


def top_entry_kernel(x_ref, g_ref, u1_ref, d2_ref, out_ref):
    lanes = 2 * out_ref.shape[3]
    pack(out_ref, 0, first_parts(x_ref, u1_ref, lanes), x_ref.shape[0])
    pack(out_ref, 7, last_parts(g_ref, d2_ref, lanes), x_ref.shape[0])


def activate(r_ref, u2_ref, slope_ref, hid_ref, tokens):
    hidden = u2_ref.shape[2]
    step = 256
    for j in range(2):
        mixed = unpack(r_ref, 0, j, tokens)
        for h in range(0, hidden, step):
            pre = tn(u2_ref[j, :, h : h + step], mixed)
            cumulative = 0.5 * (1.0 + lax.erf(pre * root_half))
            hid_ref[j, h : h + step] = (pre * cumulative).astype(bf16)
            density = jnp.exp(-0.5 * pre * pre) * norm_density
            slope_ref[j, h : h + step] = (cumulative + pre * density).astype(bf16)


def forward_kernel(r_ref, d1_ref, u2_ref, out_ref, slope_ref, hid_ref, *, tokens):
    activate(r_ref, u2_ref, slope_ref, hid_ref, tokens)
    pack(out_ref, 0, [tn(d1_ref[j], hid_ref[j]) for j in range(2)], tokens)


def top_kernel(
    r_ref, d1_ref, u2_ref, out_ref, slope_ref, hid_ref, mixed_ref, gd_ref, *, tokens
):
    activate(r_ref, u2_ref, slope_ref, hid_ref, tokens)
    mixed_ref[...] = r_ref[:, :7]
    gd_ref[...] = r_ref[:, 7:]
    backward(gd_ref, slope_ref, d1_ref, u2_ref, out_ref, tokens)


def backward(r_ref, slope_ref, d1_ref, u2_ref, out_ref, tokens):
    step = 256
    mixes = []
    for j in range(2):
        grad_down = unpack(r_ref, 0, j, tokens)
        grads = []
        for h in range(0, d1_ref.shape[1], step):
            grad_hidden = nn(d1_ref[j, h : h + step], grad_down)
            grads.append((grad_hidden * slope_ref[j, h : h + step]).astype(bf16))
        mixes.append(nn(u2_ref[j], jnp.concatenate(grads, axis=0)))
    pack(out_ref, 0, mixes, tokens)


def middle_kernel(r_ref, slope_ref, d1_ref, u2_ref, out_ref, *, tokens):
    backward(r_ref, slope_ref, d1_ref, u2_ref, out_ref, tokens)


def down_kernel(hid_ref, d1_ref, out_ref, *, tokens):
    pack(out_ref, 0, [tn(d1_ref[j], hid_ref[j]) for j in range(2)], tokens)


def head_kernel(g_ref, d2_ref, out_ref):
    pack(out_ref, 0, last_parts(g_ref, d2_ref, 2 * out_ref.shape[3]), g_ref.shape[0])


def tail_kernel(r_ref, g_ref, u1_ref, out_ref):
    tokens = g_ref.shape[0]
    width = u1_ref.shape[1]
    for i in range(2):
        cols = slice(i * width, (i + 1) * width)
        acts = nn(u1_ref[i], unpack(r_ref, 0, i, tokens)).T[:tokens]
        out_ref[:, cols] = (g_ref[:, cols].astype(f32) + acts).astype(bf16)


def main_terms_kernel(
    dp_ref, last_ref, g_ref, hid_ref, gd_ref, mixed_ref, slope_ref, d1_ref, *rest
):
    outs, low_ref = rest[:-1], rest[-1]
    tokens = g_ref.shape[0]
    hidden, lanes = hid_ref.shape[1:]
    width = g_ref.shape[1] // 2
    shares = len(outs)
    part, deep = width // shares, hidden // shares
    half = outs[0].shape[0] // 2

    def put(k, base, value):
        outs[k][base : base + value.shape[0]] = value.astype(bf16)

    def turned(n):
        spans = []
        for k in range(shares):
            d = lax.rem(dp_ref[0] + k, shares)
            spans.append(low_ref[n, pl.ds(pl.multiple_of(d * part, part), part)])
        return jnp.concatenate(spans, axis=0)

    for j in range(2):
        g = padded(g_ref[:, j * width : (j + 1) * width], lanes)
        grad_down = unpack(gd_ref, 0, j, tokens)
        low_ref[0] = unpack(last_ref, 0, j, tokens)
        low_ref[1] = unpack(mixed_ref, 0, j, tokens)
        start = j * half
        lows = nn(turned(0), g)
        for k in range(shares):
            put(k, start, lows[k * part : (k + 1) * part])
        for k in range(shares):
            d = lax.rem(dp_ref[0] + k, shares)
            rows = hid_ref[j, pl.ds(pl.multiple_of(d * deep, deep), deep)]
            put(k, start + part, nt(rows, grad_down))
        mixed = turned(1)
        for q in range(hidden // width):
            span = slice(q * width, (q + 1) * width)
            grad_hidden = nn(d1_ref[j, span], grad_down)
            grads = (grad_hidden * slope_ref[j, span]).astype(bf16)
            terms = nt(mixed, grads)
            for k in range(shares):
                put(k, start + part + deep + q * part, terms[k * part : (k + 1) * part])


def first_terms_kernel(dp_ref, x_ref, gf_ref, *rest):
    outs, xt_ref = rest[:-1], rest[-1]
    shares = len(outs)
    width, lanes = xt_ref.shape[1:]
    part = width // shares
    for i in range(2):
        grad_first = unpack(gf_ref, 0, i, x_ref.shape[0])
        rows = padded(x_ref[:, i * width : (i + 1) * width], lanes)
        xt_ref[i] = rows.astype(f32).T.astype(bf16)
        for k in range(shares):
            d = lax.rem(dp_ref[0] + k, shares)
            rows = xt_ref[i, pl.ds(pl.multiple_of(d * part, part), part)]
            outs[k][i * part : (i + 1) * part] = nt(rows, grad_first).astype(bf16)


def main_sum_kernel(*refs, factor):
    parts, (second_ref, down_ref, last_ref) = refs[:-3], refs[-3:]
    part, width = last_ref.shape[1:]
    deep = down_ref.shape[1]
    hidden = second_ref.shape[2]
    half = parts[0].shape[0] // 2

    def total(base, count):
        value = parts[0][base : base + count].astype(f32)
        for ref in parts[1:]:
            value = value + ref[base : base + count].astype(f32)
        return value * factor

    for j in range(2):
        start = j * half
        last_ref[j] = total(start, part)
        down_ref[j] = total(start + part, deep)
        for q in range(hidden // width):
            at = start + part + deep + q * part
            second_ref[j, :, q * width : (q + 1) * width] = total(at, part)


def first_sum_kernel(*refs, factor):
    parts, out_ref = refs[:-1], refs[-1]
    part = out_ref.shape[1]
    for i in range(2):
        value = parts[0][i * part : (i + 1) * part].astype(f32)
        for ref in parts[1:]:
            value = value + ref[i * part : (i + 1) * part].astype(f32)
        out_ref[i] = value * factor


def shuffle(value):
    return lax.all_to_all(value, "tensor", split_axis=0, concat_axis=0, tiled=True)


def spread(chunks):
    shares = len(chunks)
    moved = [chunks[0]]
    for k in range(1, shares):
        pairs = [(i, (i + k) % shares) for i in range(shares)]
        moved.append(lax.ppermute(chunks[k], "dp", pairs))
    return moved


def body(inputs, cotangent, up_first, up_second, down_first, down_second):
    x, u1, u2, d1, d2 = (inputs[0], up_first[0], up_second[0], down_first[0], down_second[0])
    tokens = x.shape[0]
    _, width, hidden = u2.shape
    peers = lax.axis_size("tensor")
    shares = lax.axis_size("dp")
    sections = lax.axis_size("pipe")
    section = lax.axis_index("pipe")
    dp_at = lax.axis_index("dp").astype(jnp.int32).reshape(1)
    factor = 1.0 / math.sqrt(tokens * shares)
    part, deep = width // shares, hidden // shares
    lanes = -(-tokens // 128) * 128
    packet = struct((peers, 7, 8, 128))
    rows = struct((tokens, 2 * width))
    tall = struct((2, hidden, lanes))
    block = 2 * 2 * width * lanes * width
    big = 2 * 2 * width * lanes * hidden

    def head(g):
        return call(head_kernel, [held(packet)], (g, d2), block)[0]

    def tail(r, g):
        return call(tail_kernel, [held(rows)], (r, g, u1), block)[0]

    def middle(gd):
        return call(
            functools.partial(middle_kernel, tokens=tokens), [held(packet)], (gd, slope, d1, u2), 2 * big
        )[0]

    def main_moved(last, g, gd):
        count = 2 * (part + deep + hidden * part // width)
        chunks = call(
            main_terms_kernel,
            [struct((count, width))] * shares,
            (dp_at, last, g, hid, gd, mixed, slope, d1),
            block + 3 * big,
            1,
            scratch=[pltpu.VMEM((2, width, lanes), bf16)],
        )
        return spread(chunks)

    def first_terms(gf):
        return call(
            first_terms_kernel,
            [struct((2 * part, width))] * shares,
            (dp_at, x, gf),
            block,
            1,
            scratch=[pltpu.VMEM((2, width, lanes), bf16)],
        )

    def main_sum(parts):
        return call(
            functools.partial(main_sum_kernel, factor=factor),
            [struct((2, part, hidden), f32), struct((2, deep, width), f32), struct((2, part, width), f32)],
            parts,
        )

    def first_sum(parts):
        return call(
            functools.partial(first_sum_kernel, factor=factor), [struct((2, part, width), f32)], parts
        )[0]

    def finish(last, g, gd, gf, out):
        moved = main_moved(last, g, gd)
        first_moved = spread(first_terms(gf))
        second, down, low = main_sum(moved)
        return out, first_sum(first_moved), second, down, low

    def top():
        sent = call(
            top_entry_kernel,
            [struct((peers, 14, 8, 128))],
            (x, cotangent, up_first[0], down_second[0]),
            2 * block,
            room=56,
        )[0]
        sent, slope, hid, mixed, gd = call(
            functools.partial(top_kernel, tokens=tokens),
            [held(packet), tall, tall, packet, packet],
            (shuffle(sent), down_first[0], up_second[0]),
            3 * big,
        )
        gf = shuffle(sent)
        out = call(tail_kernel, [held(rows)], (gf, cotangent, up_first[0]), block)[0]
        return out, slope, hid, mixed, gf, gd

    def rest():
        sent = call(entry_kernel, [packet], (x, up_first[0]), block, room=56)[0]
        mixed = shuffle(sent)
        sent, slope, hid = call(
            functools.partial(forward_kernel, tokens=tokens),
            [held(packet), tall, tall],
            (mixed, down_first[0], up_second[0]),
            2 * big,
        )
        last = lax.cond(section == 2, lambda: sent, lambda: shuffle(sent))
        return jnp.zeros(rows.shape, bf16), slope, hid, mixed, last, jnp.zeros(packet.shape, bf16)

    out3, slope, hid, mixed, r1, gd3 = lax.cond(section == sections - 1, top, rest)
    u1, d2, d1, u2 = call(stage_kernel, [held(u1), held(d2), held(d1), held(u2)], (u1, d2, d1, u2))
    u1, d2, d1, u2 = near(u1), near(d2), near(d1), near(u2)

    def chain(g):
        gd = shuffle(head(g))
        gf = shuffle(middle(gd))
        return tail(gf, g), gd, gf

    def hand(value, source):
        return lax.ppermute(value, "pipe", [(source, source - 1)])

    g2 = hand(out3, 3)
    g2_near = near(g2)
    saved2 = lax.cond(section == 2, lambda: chain(g2_near), lambda: (out3, gd3, r1))
    g1 = hand(saved2[0], 2)
    g1_near = near(g1)
    saved = lax.cond(section == 1, lambda: chain(g1_near), lambda: saved2)
    g0 = near(hand(saved[0], 1))

    def last_turn():
        gd = shuffle(head(g0))
        sent = middle(gd)
        moved = main_moved(r1, g0, gd)
        gf = shuffle(sent)
        first_moved = spread(first_terms(gf))
        out = tail(gf, g0)
        second, down, low = main_sum(moved)
        return out, first_sum(first_moved), second, down, low

    def close(last):
        out, gd, gf = saved
        g = jnp.where(section == 3, cotangent, jnp.where(section == 2, g2, g1))
        return finish(last, g, gd, gf, out)

    def close_late():
        sent = call(functools.partial(down_kernel, tokens=tokens), [packet], (hid, d1), big)[0]
        return close(shuffle(sent))

    branch = jnp.where(section == 0, 0, jnp.where(section == 1, 1, 2))
    done = lax.switch(branch, [last_turn, lambda: close(r1), close_late])
    out, first, second, down, low = done
    return (out[None], first[None], second[None], down[None], low[None])


def solution(mesh):
    return jax.shard_map(
        body,
        mesh=mesh,
        in_specs=(
            P("pipe", "dp", "tensor"),
            P("dp", "tensor"),
            P("pipe", "tensor", None, None),
            P("pipe", "tensor", None, None),
            P("pipe", "tensor", None, None),
            P("pipe", "tensor", None, None),
        ),
        out_specs=(
            P("pipe", "dp", "tensor"),
            P("pipe", "tensor", "dp", None),
            P("pipe", "tensor", "dp", None),
            P("pipe", "tensor", "dp", None),
            P("pipe", "tensor", "dp", None),
        ),
        check_vma=False,
    )
```

profile of v0, /device:TPU:8, one launch (start us, length us, event | category | flops | bytes accessed | tf_op | source)
XLA Modules:
  0.0 152.0 jit_solution(95866227146019665)
XLA Ops:
  0.6 37.8 %conditional.5 = (bf16[224,512]{1,0:T(8,128)(2,1)S(1)}, bf16[2,1024,256]{2,1,0:T(8,128)(2,1)}, bf16[2,1024,256]{2,1,0:T(8,128)(2,1)}, bf16[16,7,8,128]{3,2,1,0:T...) conditional(s32[]{:T(128)} %convert_element_type.14, ...), branch_computations={%region_0.0_spmd, %region_3.0_spmd} | conditional | flops 1006632960 | bytes 19464352 | solution.py:412
  0.7 2.2 %branch_0_fun.9 = bf16[16,7,8,128]{3,2,1,0:T(8,128)(2,1)} custom-call(bf16[224,512]{1,0:T(8,128)(2,1)} %get-tuple-element.141.x_ref, bf16[2,256,256]{2,1,0:T(8,128)(2,1)} %bitcast.37), custom_call_target="tpu_custom_call" | custom-call | flops 67108864 | bytes 720896 | tf_op jit(solution)/shard_map/cond/branch_0_fun/pallas_call | solution.py:94
  2.9 9.0 %all-to-all-start.1 = ((bf16[16,7,8,128]{3,2,1,0:T(8,128)(2,1)}), bf16[16,7,8,128]{3,2,1,0:T(8,128)(2,1)S(1)}, u32[]{:S(2)}, u32[]{:S(2)}) async-start(bf16[16,7,8,128]{3,2,1,0:T(8,128)(2,1)} %branch_0_fun.9), calls=%async_computation.1 | async-start | bytes 458752 | tf_op jit(solution)/shard_map/cond/branch_0_fun/all_to_all | solution.py:301
  11.9 7.9 %all-to-all-done.1.r_ref = bf16[16,7,8,128]{3,2,1,0:T(8,128)(2,1)S(1)} async-done(((bf16[16,7,8,128]{3,2,1,0:T(8,128)(2,1)}), bf16[16,7,8,128]{3,2,1,0:T(8,128)(2,1)S(1)}, u32[]{:S(2)}, u32[]{:S(2)}) %all-to-all-start.1) | async-done | bytes 229408 | tf_op jit(solution)/shard_map/cond/branch_0_fun/all_to_all | solution.py:301
  19.8 3.9 %branch_0_fun.10 = (bf16[16,7,8,128]{3,2,1,0:T(8,128)(2,1)}, bf16[2,1024,256]{2,1,0:T(8,128)(2,1)}, bf16[2,1024,256]{2,1,0:T(8,128)(2,1)}) custom-call(bf16[16,7,8,128]{3,2,1,0:T(8,128)(2,1)S(1)} %all-to-all-done.1.r_ref, bf16[2,1024,256]{2,1,0:T(8,128)(2,1)S(1)} %bitcast.31, bf16[2,256,1024]{2,1,0:T(8,128)(2,1)} %bitcast.34), custom_call_target="tpu_custom_call" | custom-call | flops 536870912 | bytes 4653056 | tf_op jit(solution)/shard_map/cond/branch_0_fun/pallas_call | solution.py:94
  23.7 14.0 %conditional = (bf16[16,7,8,128]{3,2,1,0:T(8,128)(2,1)}) conditional(s32[]{:T(128)} %convert_element_type.8, bf16[16,7,8,128]{3,2,1,0:T(8,128)(2,1)} %get-tuple-element.148, bf16[16,7,8,128]{3,2,1,0:T(8,128)(2,1)} %get-tuple-element.148), branch_computations={%region_1.0_spmd, %region_2.0_spmd} | conditional | bytes 917512 | solution.py:409
  23.7 0.9 copy.53
  24.6 13.0 %all_to_all.44 = bf16[16,7,8,128]{3,2,1,0:T(8,128)(2,1)} all-to-all(bf16[16,7,8,128]{3,2,1,0:T(8,128)(2,1)S(1)} %copy.53), channel_id=1, replica_groups=mesh['dp'=4,'pipe'=4,'tensor'=16] {'tensor'}, dimensions={0} | all-to-all | bytes 458752 | tf_op jit(solution)/shard_map/cond/branch_0_fun/cond/branch_0_fun/all_to_all | solution.py:301
  39.1 2.0 %shard_map.101 = (bf16[2,256,256]{2,1,0:T(8,128)(2,1)S(1)}, bf16[2,256,256]{2,1,0:T(8,128)(2,1)S(1)}, bf16[2,1024,256]{2,1,0:T(8,128)(2,1)S(1)}, bf16[2,256,1024]{2,1,0:T(8,128)(2,1)S(1)}) custom-call(bf16[2,256,256]{2,1,0:T(8,128)(2,1)} %bitcast.36, bf16[2,256,256]{2,1,0:T(8,128)(2,1)} %bitcast.40, bf16[2,1024,256]{2,1,0:T(8,128)(2,1)} %bitcast.30, ...), custom_call_target="tpu_custom_call" | custom-call | bytes 5242880 | tf_op jit(solution)/shard_map/pallas_call | solution.py:94
  41.1 1.6 %conditional.6 = (bf16[224,512]{1,0:T(8,128)(2,1)S(1)}, bf16[16,7,8,128]{3,2,1,0:T(8,128)(2,1)}, bf16[16,7,8,128]{3,2,1,0:T(8,128)(2,1)}) conditional(s32[]{:T(128)} %convert_element_type.13, (bf16[224,512]{1,0:T(8,128)(2,1)S(1)}, bf16[16,7,8,128]{3,2,1,0:T(8,128)(2,1)}, bf16[16,7,8,128]{3,2,1,0:T(8,128)(2,1)}) %tuple.55, ...), branch_computations={%region_4.0_spmd, %region_5.0_spmd} | conditional | flops 671088640 | bytes 7110708 | solution.py:426
  41.1 1.6 %copy.27 = bf16[16,7,8,128]{3,2,1,0:T(8,128)(2,1)} copy(bf16[16,7,8,128]{3,2,1,0:T(8,128)(2,1)} %get-tuple-element.300) | data formatting | bytes 458752 | tf_op jit(solution)/shard_map/cond
  43.4 1.3 collective-permute-start.20
  44.7 61.0 %collective-permute-done.20 = bf16[224,512]{1,0:T(8,128)(2,1)S(1)} collective-permute-done((bf16[224,512]{1,0:T(8,128)(2,1)S(1)}, bf16[224,512]{1,0:T(8,128)(2,1)S(1)}, u32[]{:S(2)}, u32[]{:S(2)}) %collective-permute-start.20) | collective-permute-done | bytes 229408 | tf_op jit(solution)/shard_map/ppermute | solution.py:422
  105.7 45.5 %conditional.8 = (f32[2,64,1024]{2,1,0:T(8,128)}, f32[2,256,256]{2,1,0:T(8,128)}, f32[2,64,256]{2,1,0:T(8,128)}, bf16[1,224,512]{2,1,0:T(8,128)(2,1)S(1)}, f32[1,2,64,256]{3,2,1,0:T(8,128)S(1)}) conditional(s32[]{:T(128)} %clamp.3, (bf16[224,512]{1,0:T(8,128)(2,1)S(1)}, bf16[2,256,256]{2,1,0:T(8,128)(2,1)S(1)}, s32[1]{0:T(128)}, ...), branch_computations={%region_8.9_spmd, %region_9.10_spmd, %region_10.11_spmd} | conditional | flops 1610612736 | bytes 30245208 | solution.py:452
  106.1 12.0 %all_to_all.51.gd_ref.r_ref = bf16[16,7,8,128]{3,2,1,0:T(8,128)(2,1)S(1)} all-to-all(bf16[16,7,8,128]{3,2,1,0:T(8,128)(2,1)S(1)} %branch_0_fun.11), channel_id=1, replica_groups=mesh['dp'=4,'pipe'=4,'tensor'=16] {'tensor'}, dimensions={0} | all-to-all | bytes 458752 | tf_op jit(solution)/shard_map/cond/branch_0_fun/all_to_all | solution.py:301
  118.1 2.7 %branch_0_fun.12 = (bf16[1152,256]{1,0:T(8,128)(2,1)S(1)}, bf16[1152,256]{1,0:T(8,128)(2,1)S(1)}, bf16[1152,256]{1,0:T(8,128)(2,1)S(1)}, bf16[1152,256]{1,0:T(8,128)(2,1)S(1)}) custom-call(s32[1]{0:T(128)} %get-tuple-element.172.dp_ref, bf16[16,7,8,128]{3,2,1,0:T(8,128)(2,1)} %get-tuple-element.173.last_ref, bf16[224,512]{1,0:T(8,128)(2,1)S(1)} %get-tuple-element.174.g_ref, ...), custom_call_target="tpu_custom_call" | custom-call | flops 872415232 | bytes 6422532 | tf_op jit(solution)/shard_map/cond/branch_0_fun/pallas_call | solution.py:94
  120.8 1.6 %collective-permute-start = (bf16[1152,256]{1,0:T(8,128)(2,1)S(1)}, bf16[1152,256]{1,0:T(8,128)(2,1)S(1)}, u32[]{:S(2)}, u32[]{:S(2)}) collective-permute-start(bf16[1152,256]{1,0:T(8,128)(2,1)S(1)} %get-tuple-element.181), channel_id=1, source_target_pairs={{0,64},{64,128},{128,192},{192,0},{1,65},{65,129},{129,193},{193,1... | collective-permute-start | bytes 1769480 | tf_op jit(solution)/shard_map/cond/branch_0_fun/ppermute | solution.py:309
  122.4 2.7 %collective-permute-start.1 = (bf16[1152,256]{1,0:T(8,128)(2,1)S(1)}, bf16[1152,256]{1,0:T(8,128)(2,1)S(1)}, u32[]{:S(2)}, u32[]{:S(2)}) collective-permute-start(bf16[1152,256]{1,0:T(8,128)(2,1)S(1)} %get-tuple-element.182), channel_id=1, source_target_pairs={{0,128},{64,192},{128,0},{192,64},{1,129},{65,193},{129,1},{193,65... | collective-permute-start | bytes 1769480 | tf_op jit(solution)/shard_map/cond/branch_0_fun/ppermute | solution.py:309
  125.1 1.4 collective-permute-start.2
  126.5 1.0 branch_0_fun.14
  127.5 12.2 %all_to_all.52.r_ref.gf_ref = bf16[16,7,8,128]{3,2,1,0:T(8,128)(2,1)S(1)} all-to-all(bf16[16,7,8,128]{3,2,1,0:T(8,128)(2,1)S(1)} %branch_0_fun.14), channel_id=1, replica_groups=mesh['dp'=4,'pipe'=4,'tensor'=16] {'tensor'}, dimensions={0} | all-to-all | bytes 458752 | tf_op jit(solution)/shard_map/cond/branch_0_fun/all_to_all | solution.py:301
  141.7 4.0 %collective-permute-done.3.refs_1_ = bf16[128,256]{1,0:T(8,128)(2,1)S(1)} collective-permute-done((bf16[128,256]{1,0:T(8,128)(2,1)S(1)}, bf16[128,256]{1,0:T(8,128)(2,1)S(1)}, u32[]{:S(2)}, u32[]{:S(2)}) %collective-permute-start.3) | collective-permute-done | bytes 65568 | tf_op jit(solution)/shard_map/cond/branch_0_fun/ppermute | solution.py:309
  146.6 3.4 %collective-permute-done.5.refs_3_ = bf16[128,256]{1,0:T(8,128)(2,1)S(1)} collective-permute-done((bf16[128,256]{1,0:T(8,128)(2,1)S(1)}, bf16[128,256]{1,0:T(8,128)(2,1)S(1)}, u32[]{:S(2)}, u32[]{:S(2)}) %collective-permute-start.5) | collective-permute-done | bytes 65568 | tf_op jit(solution)/shard_map/cond/branch_0_fun/ppermute | solution.py:309
  150.1 1.2 branch_0_fun.13
  (31 shorter events, 6.1 us)
Async XLA Ops:
  0.6 19.1 %copy-start.13 = (bf16[1,2,1024,256]{3,2,1,0:T(8,128)(2,1)S(1)}, bf16[1,2,1024,256]{3,2,1,0:T(8,128)(2,1)}, u32[]{:S(2)}) copy-start(bf16[1,2,1024,256]{3,2,1,0:T(8,128)(2,1)} %get-tuple-element.143) | copy-start | bytes 3145732 | tf_op jit(solution)/shard_map/cond
  2.9 16.9 %all-to-all-start.1 = ((bf16[16,7,8,128]{3,2,1,0:T(8,128)(2,1)}), bf16[16,7,8,128]{3,2,1,0:T(8,128)(2,1)S(1)}, u32[]{:S(2)}, u32[]{:S(2)}) async-start(bf16[16,7,8,128]{3,2,1,0:T(8,128)(2,1)} %branch_0_fun.9), calls=%async_computation.1 | async-start | bytes 458752 | tf_op jit(solution)/shard_map/cond/branch_0_fun/all_to_all | solution.py:301
  19.8 3.9 %copy-start.8 = (bf16[16,7,8,128]{3,2,1,0:T(8,128)(2,1)}, bf16[16,7,8,128]{3,2,1,0:T(8,128)(2,1)S(1)}, u32[]{:S(2)}) copy-start(bf16[16,7,8,128]{3,2,1,0:T(8,128)(2,1)S(1)} %all-to-all-done.1.r_ref) | copy-start | bytes 688132 | tf_op jit(solution)/shard_map/cond
  38.4 2.7 %collective-permute-start.18 = (bf16[224,512]{1,0:T(8,128)(2,1)S(1)}, bf16[224,512]{1,0:T(8,128)(2,1)S(1)}, u32[]{:S(2)}, u32[]{:S(2)}) collective-permute-start(bf16[224,512]{1,0:T(8,128)(2,1)S(1)} %get-tuple-element.267), channel_id=1, source_target_pairs={{48,32},{49,33},{50,34},{51,35},{52,36},{53,37},{54,38},{55,39},{5... | collective-permute-start | bytes 688136 | tf_op jit(solution)/shard_map/ppermute | solution.py:422
  39.1 2.0 %copy-start = (bf16[2,1024,256]{2,1,0:T(8,128)(2,1)S(1)}, bf16[2,1024,256]{2,1,0:T(8,128)(2,1)}, u32[]{:S(2)}) copy-start(bf16[2,1024,256]{2,1,0:T(8,128)(2,1)} %get-tuple-element.271) | copy-start | bytes 3145732
  42.7 0.7 collective-permute-start.19
  43.4 62.3 %collective-permute-start.20 = (bf16[224,512]{1,0:T(8,128)(2,1)S(1)}, bf16[224,512]{1,0:T(8,128)(2,1)S(1)}, u32[]{:S(2)}, u32[]{:S(2)}) collective-permute-start(bf16[224,512]{1,0:T(8,128)(2,1)S(1)} %get-tuple-element.276), channel_id=1, source_target_pairs={{16,0},{17,1},{18,2},{19,3},{20,4},{21,5},{22,6},{23,7},{24,8},{25... | collective-permute-start | bytes 688136 | tf_op jit(solution)/shard_map/ppermute | solution.py:422
  105.7 12.4 %copy-start.2 = (bf16[2,1024,256]{2,1,0:T(8,128)(2,1)S(1)}, bf16[2,1024,256]{2,1,0:T(8,128)(2,1)}, u32[]{:S(2)}) copy-start(bf16[2,1024,256]{2,1,0:T(8,128)(2,1)} %get-tuple-element.178.slope_ref) | copy-start | bytes 3145732 | tf_op jit(solution)/shard_map/cond
  120.8 29.3 %collective-permute-start = (bf16[1152,256]{1,0:T(8,128)(2,1)S(1)}, bf16[1152,256]{1,0:T(8,128)(2,1)S(1)}, u32[]{:S(2)}, u32[]{:S(2)}) collective-permute-start(bf16[1152,256]{1,0:T(8,128)(2,1)S(1)} %get-tuple-element.181), channel_id=1, source_target_pairs={{0,64},{64,128},{128,192},{192,0},{1,65},{65,129},{129,193},{193,1... | collective-permute-start | bytes 1769480 | tf_op jit(solution)/shard_map/cond/branch_0_fun/ppermute | solution.py:309
  122.4 27.7 %collective-permute-start.1 = (bf16[1152,256]{1,0:T(8,128)(2,1)S(1)}, bf16[1152,256]{1,0:T(8,128)(2,1)S(1)}, u32[]{:S(2)}, u32[]{:S(2)}) collective-permute-start(bf16[1152,256]{1,0:T(8,128)(2,1)S(1)} %get-tuple-element.182), channel_id=1, source_target_pairs={{0,128},{64,192},{128,0},{192,64},{1,129},{65,193},{129,1},{193,65... | collective-permute-start | bytes 1769480 | tf_op jit(solution)/shard_map/cond/branch_0_fun/ppermute | solution.py:309
  125.1 25.0 %collective-permute-start.2 = (bf16[1152,256]{1,0:T(8,128)(2,1)S(1)}, bf16[1152,256]{1,0:T(8,128)(2,1)S(1)}, u32[]{:S(2)}, u32[]{:S(2)}) collective-permute-start(bf16[1152,256]{1,0:T(8,128)(2,1)S(1)} %get-tuple-element.183), channel_id=1, source_target_pairs={{0,192},{64,0},{128,64},{192,128},{1,193},{65,1},{129,65},{193,129... | collective-permute-start | bytes 1769480 | tf_op jit(solution)/shard_map/cond/branch_0_fun/ppermute | solution.py:309
  127.5 12.2 %copy-start.10 = (bf16[224,512]{1,0:T(8,128)(2,1)S(1)}, bf16[224,512]{1,0:T(8,128)(2,1)}, u32[]{:S(2)}) copy-start(bf16[224,512]{1,0:T(8,128)(2,1)} %get-tuple-element.189.x_ref) | copy-start | bytes 688132 | tf_op jit(solution)/shard_map/cond
  140.2 5.6 %collective-permute-start.3 = (bf16[128,256]{1,0:T(8,128)(2,1)S(1)}, bf16[128,256]{1,0:T(8,128)(2,1)S(1)}, u32[]{:S(2)}, u32[]{:S(2)}) collective-permute-start(bf16[128,256]{1,0:T(8,128)(2,1)S(1)} %get-tuple-element.191), channel_id=1, source_target_pairs={{0,64},{64,128},{128,192},{192,0},{1,65},{65,129},{129,193},{193,1... | collective-permute-start | bytes 196616 | tf_op jit(solution)/shard_map/cond/branch_0_fun/ppermute | solution.py:309
  140.8 5.8 %collective-permute-start.4 = (bf16[128,256]{1,0:T(8,128)(2,1)S(1)}, bf16[128,256]{1,0:T(8,128)(2,1)S(1)}, u32[]{:S(2)}, u32[]{:S(2)}) collective-permute-start(bf16[128,256]{1,0:T(8,128)(2,1)S(1)} %get-tuple-element.192), channel_id=1, source_target_pairs={{0,128},{64,192},{128,0},{192,64},{1,129},{65,193},{129,1},{193,65... | collective-permute-start | bytes 196616 | tf_op jit(solution)/shard_map/cond/branch_0_fun/ppermute | solution.py:309
  145.7 4.3 %collective-permute-start.5 = (bf16[128,256]{1,0:T(8,128)(2,1)S(1)}, bf16[128,256]{1,0:T(8,128)(2,1)S(1)}, u32[]{:S(2)}, u32[]{:S(2)}) collective-permute-start(bf16[128,256]{1,0:T(8,128)(2,1)S(1)} %get-tuple-element.193), channel_id=1, source_target_pairs={{0,192},{64,0},{128,64},{192,128},{1,193},{65,1},{129,65},{193,129... | collective-permute-start | bytes 196616 | tf_op jit(solution)/shard_map/cond/branch_0_fun/ppermute | solution.py:309
  151.2 0.7 copy-start.18
where the time goes:
time: 153 us; the launch traced here: 152 us
  waiting for transfers between devices  76.8 us (50%)
  blocking collectives  37.2 us (24%)
  starting transfers between devices  18.9 us (12%)
  Pallas kernels  14.1 us (9%)
  local copies, waits for them, and re-layouts  4.11 us (3%)
    ppermute x3, waiting for transfers between devices, hand(): return lax.ppermute(value, 'pipe', [(source, source - 1)])  61 us
    all_to_all x3, blocking collectives, shuffle(): lax.all_to_all(value, 'tensor', split_axis=0, concat_axis=0, tiled=True)  37.2 us
    pallas_call x10, Pallas kernels, call(): pl.pallas_call(body, out_shape=outs, scratch_shapes=scratch, in_specs=spe...  14.1 us
    all_to_all x1, starting transfers between devices, shuffle(): lax.all_to_all(value, 'tensor', split_axis=0, concat_axis=0, tiled=True)  8.99 us
    ppermute x6, waiting for transfers between devices, spread(): moved.append(lax.ppermute(chunks[k], 'dp', pairs))  7.91 us
    all_to_all x1, waiting for transfers between devices, shuffle(): lax.all_to_all(value, 'tensor', split_axis=0, concat_axis=0, tiled=True)  7.86 us
    ppermute x6, starting transfers between devices, spread(): moved.append(lax.ppermute(chunks[k], 'dp', pairs))  7.29 us
  transfers between devices with their start and end apart: 10, of which 5 were waited for; matrix products, arithmetic and copies ran while one was open for 0% of the time, Pallas kernels for 2%

commit v1 on v0

--- a/solution.py
+++ b/solution.py
@@ -81,11 +81,19 @@
     return pltpu.with_memory_space_constraint(value, pltpu.VMEM)
 
 
+def far(value):
+    return pltpu.with_memory_space_constraint(value, pltpu.HBM)
+
+
 def held(value):
     return pltpu.VMEM(value.shape, value.dtype)
 
 
-def call(body, outs, args, flops=0, scalars=0, scratch=(), room=12):
+def away(value):
+    return pltpu.HBM(value.shape, value.dtype)
+
+
+def call(body, outs, args, flops=0, scalars=0, scratch=(), room=8):
     moved = sum(a.size * a.dtype.itemsize for a in args) + sum(
         math.prod(o.shape) * o.dtype.itemsize for o in outs
     )
@@ -370,7 +378,9 @@
 
     def first_sum(parts):
         return call(
-            functools.partial(first_sum_kernel, factor=factor), [struct((2, part, width), f32)], parts
+            functools.partial(first_sum_kernel, factor=factor),
+            [away(struct((2, part, width), f32))],
+            parts,
         )[0]
 
     def finish(last, g, gd, gf, out):
@@ -382,10 +392,9 @@
     def top():
         sent = call(
             top_entry_kernel,
-            [struct((peers, 14, 8, 128))],
-            (x, cotangent, up_first[0], down_second[0]),
+            [held(struct((peers, 14, 8, 128)))],
+            (far(x), far(cotangent), far(up_first[0]), far(down_second[0])),
             2 * block,
-            room=56,
         )[0]
         sent, slope, hid, mixed, gd = call(
             functools.partial(top_kernel, tokens=tokens),
@@ -398,7 +407,7 @@
         return out, slope, hid, mixed, gf, gd
 
     def rest():
-        sent = call(entry_kernel, [packet], (x, up_first[0]), block, room=56)[0]
+        sent = call(entry_kernel, [held(packet)], (far(x), far(up_first[0])), block)[0]
         mixed = shuffle(sent)
         sent, slope, hid = call(
             functools.partial(forward_kernel, tokens=tokens),
@@ -410,7 +419,9 @@
         return jnp.zeros(rows.shape, bf16), slope, hid, mixed, last, jnp.zeros(packet.shape, bf16)
 
     out3, slope, hid, mixed, r1, gd3 = lax.cond(section == sections - 1, top, rest)
-    u1, d2, d1, u2 = call(stage_kernel, [held(u1), held(d2), held(d1), held(u2)], (u1, d2, d1, u2))
+    u1, d2, d1, u2 = call(
+        stage_kernel, [held(u1), held(d2), held(d1), held(u2)], (u1, d2, d1, u2)
+    )
     u1, d2, d1, u2 = near(u1), near(d2), near(d1), near(u2)
 
     def chain(g):
@@ -435,14 +446,15 @@
         moved = main_moved(r1, g0, gd)
         gf = shuffle(sent)
         first_moved = spread(first_terms(gf))
-        out = tail(gf, g0)
         second, down, low = main_sum(moved)
-        return out, first_sum(first_moved), second, down, low
+        out = call(tail_kernel, [away(rows)], (gf, g0, u1), block)[0]
+        first = first_sum(first_moved)
+        return out, first, second, down, low
 
     def close(last):
         out, gd, gf = saved
         g = jnp.where(section == 3, cotangent, jnp.where(section == 2, g2, g1))
-        return finish(last, g, gd, gf, out)
+        return finish(last, g, gd, gf, call(stage_kernel, [away(rows)], (out,))[0])
 
     def close_late():
         sent = call(functools.partial(down_kernel, tokens=tokens), [packet], (hid, d1), big)[0]

time: 153 us -> 152 us (level)
  waiting for transfers between devices: 76.8 us -> 75.1 us
  transfers between devices with their start and end apart: 10 -> 10, of which waited for: 5 -> 4; matrix products, arithmetic and copies ran while one was open for 0% -> 0% of each run, Pallas kernels for 2% -> 3%
where the time goes in v1:
time: 152 us; the launch traced here: 151 us
  waiting for transfers between devices  75.1 us (49%)
  blocking collectives  37.3 us (25%)
  starting transfers between devices  18.9 us (12%)
  Pallas kernels  15.4 us (10%)
  local copies, waits for them, and re-layouts  3.4 us (2%)
    ppermute x3, waiting for transfers between devices, hand(): return lax.ppermute(value, 'pipe', [(source, source - 1)])  60 us
    all_to_all x3, blocking collectives, shuffle(): lax.all_to_all(value, 'tensor', split_axis=0, concat_axis=0, tiled=True)  37.3 us
    pallas_call x10, Pallas kernels, call(): pl.pallas_call(body, out_shape=outs, scratch_shapes=scratch, in_specs=spe...  15.4 us
    all_to_all x1, starting transfers between devices, shuffle(): lax.all_to_all(value, 'tensor', split_axis=0, concat_axis=0, tiled=True)  8.99 us
    all_to_all x1, waiting for transfers between devices, shuffle(): lax.all_to_all(value, 'tensor', split_axis=0, concat_axis=0, tiled=True)  7.86 us
    ppermute x6, starting transfers between devices, spread(): moved.append(lax.ppermute(chunks[k], 'dp', pairs))  7.28 us
    ppermute x6, waiting for transfers between devices, spread(): moved.append(lax.ppermute(chunks[k], 'dp', pairs))  7.23 us
  transfers between devices with their start and end apart: 10, of which 4 were waited for; matrix products, arithmetic and copies ran while one was open for 0% of the time, Pallas kernels for 3%

profile of v1, /device:TPU:8, one launch (start us, length us, event | category | flops | bytes accessed | tf_op | source)
XLA Modules:
  0.0 150.9 jit_solution(11840717348951665379)
XLA Ops:
  0.6 37.7 %conditional.5 = (bf16[224,512]{1,0:T(8,128)(2,1)S(1)}, bf16[2,1024,256]{2,1,0:T(8,128)(2,1)}, bf16[2,1024,256]{2,1,0:T(8,128)(2,1)}, bf16[16,7,8,128]{3,2,1,0:T...) conditional(s32[]{:T(128)} %convert_element_type.14, ...), branch_computations={%region_0.0_spmd, %region_3.0_spmd} | conditional | flops 1006632960 | bytes 19464352 | solution.py:421
  0.7 2.2 %branch_0_fun.9 = bf16[16,7,8,128]{3,2,1,0:T(8,128)(2,1)} custom-call(bf16[224,512]{1,0:T(8,128)(2,1)} %get-tuple-element.141.x_ref, bf16[2,256,256]{2,1,0:T(8,128)(2,1)} %bitcast.34), custom_call_target="tpu_custom_call" | custom-call | flops 67108864 | bytes 720896 | tf_op jit(solution)/shard_map/cond/branch_0_fun/pallas_call | solution.py:102
  2.9 9.0 %all-to-all-start.1 = ((bf16[16,7,8,128]{3,2,1,0:T(8,128)(2,1)}), bf16[16,7,8,128]{3,2,1,0:T(8,128)(2,1)S(1)}, u32[]{:S(2)}, u32[]{:S(2)}) async-start(bf16[16,7,8,128]{3,2,1,0:T(8,128)(2,1)} %branch_0_fun.9), calls=%async_computation.1 | async-start | bytes 458752 | tf_op jit(solution)/shard_map/cond/branch_0_fun/all_to_all | solution.py:309
  11.9 7.9 %all-to-all-done.1.r_ref = bf16[16,7,8,128]{3,2,1,0:T(8,128)(2,1)S(1)} async-done(((bf16[16,7,8,128]{3,2,1,0:T(8,128)(2,1)}), bf16[16,7,8,128]{3,2,1,0:T(8,128)(2,1)S(1)}, u32[]{:S(2)}, u32[]{:S(2)}) %all-to-all-start.1) | async-done | bytes 229408 | tf_op jit(solution)/shard_map/cond/branch_0_fun/all_to_all | solution.py:309
  19.8 3.9 %branch_0_fun.10 = (bf16[16,7,8,128]{3,2,1,0:T(8,128)(2,1)}, bf16[2,1024,256]{2,1,0:T(8,128)(2,1)}, bf16[2,1024,256]{2,1,0:T(8,128)(2,1)}) custom-call(bf16[16,7,8,128]{3,2,1,0:T(8,128)(2,1)S(1)} %all-to-all-done.1.r_ref, bf16[2,1024,256]{2,1,0:T(8,128)(2,1)S(1)} %bitcast.28, bf16[2,256,1024]{2,1,0:T(8,128)(2,1)} %bitcast.31), custom_call_target="tpu_custom_call" | custom-call | flops 536870912 | bytes 4653056 | tf_op jit(solution)/shard_map/cond/branch_0_fun/pallas_call | solution.py:102
  23.7 14.0 %conditional = (bf16[16,7,8,128]{3,2,1,0:T(8,128)(2,1)}) conditional(s32[]{:T(128)} %convert_element_type.8, bf16[16,7,8,128]{3,2,1,0:T(8,128)(2,1)} %get-tuple-element.148, bf16[16,7,8,128]{3,2,1,0:T(8,128)(2,1)} %get-tuple-element.148), branch_computations={%region_1.0_spmd, %region_2.0_spmd} | conditional | bytes 917512 | solution.py:418
  24.6 13.0 %all_to_all.44 = bf16[16,7,8,128]{3,2,1,0:T(8,128)(2,1)} all-to-all(bf16[16,7,8,128]{3,2,1,0:T(8,128)(2,1)S(1)} %copy.52), channel_id=1, replica_groups=mesh['dp'=4,'pipe'=4,'tensor'=16] {'tensor'}, dimensions={0} | all-to-all | bytes 458752 | tf_op jit(solution)/shard_map/cond/branch_0_fun/cond/branch_0_fun/all_to_all | solution.py:309
  39.1 2.0 %shard_map.101 = (bf16[2,256,256]{2,1,0:T(8,128)(2,1)S(1)}, bf16[2,256,256]{2,1,0:T(8,128)(2,1)S(1)}, bf16[2,1024,256]{2,1,0:T(8,128)(2,1)S(1)}, bf16[2,256,1024]{2,1,0:T(8,128)(2,1)S(1)}) custom-call(bf16[2,256,256]{2,1,0:T(8,128)(2,1)} %bitcast.33, bf16[2,256,256]{2,1,0:T(8,128)(2,1)} %bitcast.37, bf16[2,1024,256]{2,1,0:T(8,128)(2,1)} %bitcast.27, ...), custom_call_target="tpu_custom_call" | custom-call | bytes 5242880 | tf_op jit(solution)/shard_map/pallas_call | solution.py:102
  41.1 1.7 %conditional.6 = (bf16[224,512]{1,0:T(8,128)(2,1)S(1)}, bf16[16,7,8,128]{3,2,1,0:T(8,128)(2,1)}, bf16[16,7,8,128]{3,2,1,0:T(8,128)(2,1)}) conditional(s32[]{:T(128)} %convert_element_type.13, (bf16[224,512]{1,0:T(8,128)(2,1)S(1)}, bf16[16,7,8,128]{3,2,1,0:T(8,128)(2,1)}, bf16[16,7,8,128]{3,2,1,0:T(8,128)(2,1)}) %tuple.55, ...), branch_computations={%region_4.0_spmd, %region_5.0_spmd} | conditional | flops 671088640 | bytes 7110708 | solution.py:437
  41.1 1.7 %copy.27 = bf16[16,7,8,128]{3,2,1,0:T(8,128)(2,1)} copy(bf16[16,7,8,128]{3,2,1,0:T(8,128)(2,1)} %get-tuple-element.300) | data formatting | bytes 458752 | tf_op jit(solution)/shard_map/cond
  43.4 1.3 collective-permute-start.20
  44.7 60.0 %collective-permute-done.20 = bf16[224,512]{1,0:T(8,128)(2,1)S(1)} collective-permute-done((bf16[224,512]{1,0:T(8,128)(2,1)S(1)}, bf16[224,512]{1,0:T(8,128)(2,1)S(1)}, u32[]{:S(2)}, u32[]{:S(2)}) %collective-permute-start.20) | collective-permute-done | bytes 229408 | tf_op jit(solution)/shard_map/ppermute | solution.py:433
  104.8 46.1 %conditional.8 = (f32[2,64,1024]{2,1,0:T(8,128)}, f32[2,256,256]{2,1,0:T(8,128)}, f32[2,64,256]{2,1,0:T(8,128)}, bf16[1,224,512]{2,1,0:T(8,128)(2,1)}, f32[1,2,64,256]{3,2,1,0:T(8,128)}) conditional(s32[]{:T(128)} %clamp.3, (bf16[224,512]{1,0:T(8,128)(2,1)S(1)}, bf16[2,256,256]{2,1,0:T(8,128)(2,1)S(1)}, s32[1]{0:T(128)}, ...), branch_computations={%region_8.9_spmd, %region_9.10_spmd, %region_10.11_spmd} | conditional | flops 1610612736 | bytes 30245208 | solution.py:464
  105.1 12.0 %all_to_all.51.gd_ref.r_ref = bf16[16,7,8,128]{3,2,1,0:T(8,128)(2,1)S(1)} all-to-all(bf16[16,7,8,128]{3,2,1,0:T(8,128)(2,1)S(1)} %branch_0_fun.11), channel_id=1, replica_groups=mesh['dp'=4,'pipe'=4,'tensor'=16] {'tensor'}, dimensions={0} | all-to-all | bytes 458752 | tf_op jit(solution)/shard_map/cond/branch_0_fun/all_to_all | solution.py:309
  117.1 2.7 %branch_0_fun.12 = (bf16[1152,256]{1,0:T(8,128)(2,1)S(1)}, bf16[1152,256]{1,0:T(8,128)(2,1)S(1)}, bf16[1152,256]{1,0:T(8,128)(2,1)S(1)}, bf16[1152,256]{1,0:T(8,128)(2,1)S(1)}) custom-call(s32[1]{0:T(128)} %get-tuple-element.172.dp_ref, bf16[16,7,8,128]{3,2,1,0:T(8,128)(2,1)} %get-tuple-element.173.last_ref, bf16[224,512]{1,0:T(8,128)(2,1)S(1)} %get-tuple-element.174.g_ref, ...), custom_call_target="tpu_custom_call" | custom-call | flops 872415232 | bytes 6422532 | tf_op jit(solution)/shard_map/cond/branch_0_fun/pallas_call | solution.py:102
  119.8 1.6 %collective-permute-start = (bf16[1152,256]{1,0:T(8,128)(2,1)S(1)}, bf16[1152,256]{1,0:T(8,128)(2,1)S(1)}, u32[]{:S(2)}, u32[]{:S(2)}) collective-permute-start(bf16[1152,256]{1,0:T(8,128)(2,1)S(1)} %get-tuple-element.181), channel_id=1, source_target_pairs={{0,64},{64,128},{128,192},{192,0},{1,65},{65,129},{129,193},{193,1... | collective-permute-start | bytes 1769480 | tf_op jit(solution)/shard_map/cond/branch_0_fun/ppermute | solution.py:317
  121.4 2.7 %collective-permute-start.1 = (bf16[1152,256]{1,0:T(8,128)(2,1)S(1)}, bf16[1152,256]{1,0:T(8,128)(2,1)S(1)}, u32[]{:S(2)}, u32[]{:S(2)}) collective-permute-start(bf16[1152,256]{1,0:T(8,128)(2,1)S(1)} %get-tuple-element.182), channel_id=1, source_target_pairs={{0,128},{64,192},{128,0},{192,64},{1,129},{65,193},{129,1},{193,65... | collective-permute-start | bytes 1769480 | tf_op jit(solution)/shard_map/cond/branch_0_fun/ppermute | solution.py:317
  124.1 1.4 collective-permute-start.2
  125.6 1.0 branch_0_fun.14
  126.5 12.2 %all_to_all.52.r_ref.gf_ref = bf16[16,7,8,128]{3,2,1,0:T(8,128)(2,1)S(1)} all-to-all(bf16[16,7,8,128]{3,2,1,0:T(8,128)(2,1)S(1)} %branch_0_fun.14), channel_id=1, replica_groups=mesh['dp'=4,'pipe'=4,'tensor'=16] {'tensor'}, dimensions={0} | all-to-all | bytes 458752 | tf_op jit(solution)/shard_map/cond/branch_0_fun/all_to_all | solution.py:309
  140.8 4.0 %collective-permute-done.3.refs_1_ = bf16[128,256]{1,0:T(8,128)(2,1)S(1)} collective-permute-done((bf16[128,256]{1,0:T(8,128)(2,1)S(1)}, bf16[128,256]{1,0:T(8,128)(2,1)S(1)}, u32[]{:S(2)}, u32[]{:S(2)}) %collective-permute-start.3) | collective-permute-done | bytes 65568 | tf_op jit(solution)/shard_map/cond/branch_0_fun/ppermute | solution.py:317
  144.8 1.0 branch_0_fun.15
  145.8 3.2 %collective-permute-done.5.refs_3_ = bf16[128,256]{1,0:T(8,128)(2,1)S(1)} collective-permute-done((bf16[128,256]{1,0:T(8,128)(2,1)S(1)}, bf16[128,256]{1,0:T(8,128)(2,1)S(1)}, u32[]{:S(2)}, u32[]{:S(2)}) %collective-permute-start.5) | collective-permute-done | bytes 65568 | tf_op jit(solution)/shard_map/cond/branch_0_fun/ppermute | solution.py:317
  149.7 1.2 branch_0_fun.13
  (28 shorter events, 6.1 us)
Async XLA Ops:
  0.6 19.1 %copy-start.13 = (bf16[1,2,1024,256]{3,2,1,0:T(8,128)(2,1)S(1)}, bf16[1,2,1024,256]{3,2,1,0:T(8,128)(2,1)}, u32[]{:S(2)}) copy-start(bf16[1,2,1024,256]{3,2,1,0:T(8,128)(2,1)} %get-tuple-element.143) | copy-start | bytes 3145732 | tf_op jit(solution)/shard_map/cond
  2.9 16.9 %all-to-all-start.1 = ((bf16[16,7,8,128]{3,2,1,0:T(8,128)(2,1)}), bf16[16,7,8,128]{3,2,1,0:T(8,128)(2,1)S(1)}, u32[]{:S(2)}, u32[]{:S(2)}) async-start(bf16[16,7,8,128]{3,2,1,0:T(8,128)(2,1)} %branch_0_fun.9), calls=%async_computation.1 | async-start | bytes 458752 | tf_op jit(solution)/shard_map/cond/branch_0_fun/all_to_all | solution.py:309
  19.8 3.9 %copy-start.8 = (bf16[16,7,8,128]{3,2,1,0:T(8,128)(2,1)}, bf16[16,7,8,128]{3,2,1,0:T(8,128)(2,1)S(1)}, u32[]{:S(2)}) copy-start(bf16[16,7,8,128]{3,2,1,0:T(8,128)(2,1)S(1)} %all-to-all-done.1.r_ref) | copy-start | bytes 688132 | tf_op jit(solution)/shard_map/cond
  38.4 2.7 %collective-permute-start.18 = (bf16[224,512]{1,0:T(8,128)(2,1)S(1)}, bf16[224,512]{1,0:T(8,128)(2,1)S(1)}, u32[]{:S(2)}, u32[]{:S(2)}) collective-permute-start(bf16[224,512]{1,0:T(8,128)(2,1)S(1)} %get-tuple-element.267), channel_id=1, source_target_pairs={{48,32},{49,33},{50,34},{51,35},{52,36},{53,37},{54,38},{55,39},{5... | collective-permute-start | bytes 688136 | tf_op jit(solution)/shard_map/ppermute | solution.py:433
  39.1 2.0 %copy-start = (bf16[2,1024,256]{2,1,0:T(8,128)(2,1)S(1)}, bf16[2,1024,256]{2,1,0:T(8,128)(2,1)}, u32[]{:S(2)}) copy-start(bf16[2,1024,256]{2,1,0:T(8,128)(2,1)} %get-tuple-element.271) | copy-start | bytes 3145732
  42.7 0.7 collective-permute-start.19
  43.4 61.3 %collective-permute-start.20 = (bf16[224,512]{1,0:T(8,128)(2,1)S(1)}, bf16[224,512]{1,0:T(8,128)(2,1)S(1)}, u32[]{:S(2)}, u32[]{:S(2)}) collective-permute-start(bf16[224,512]{1,0:T(8,128)(2,1)S(1)} %get-tuple-element.276), channel_id=1, source_target_pairs={{16,0},{17,1},{18,2},{19,3},{20,4},{21,5},{22,6},{23,7},{24,8},{25... | collective-permute-start | bytes 688136 | tf_op jit(solution)/shard_map/ppermute | solution.py:433
  104.8 12.4 %copy-start.2 = (bf16[2,1024,256]{2,1,0:T(8,128)(2,1)S(1)}, bf16[2,1024,256]{2,1,0:T(8,128)(2,1)}, u32[]{:S(2)}) copy-start(bf16[2,1024,256]{2,1,0:T(8,128)(2,1)} %get-tuple-element.178.slope_ref) | copy-start | bytes 3145732 | tf_op jit(solution)/shard_map/cond
  119.8 29.9 %collective-permute-start = (bf16[1152,256]{1,0:T(8,128)(2,1)S(1)}, bf16[1152,256]{1,0:T(8,128)(2,1)S(1)}, u32[]{:S(2)}, u32[]{:S(2)}) collective-permute-start(bf16[1152,256]{1,0:T(8,128)(2,1)S(1)} %get-tuple-element.181), channel_id=1, source_target_pairs={{0,64},{64,128},{128,192},{192,0},{1,65},{65,129},{129,193},{193,1... | collective-permute-start | bytes 1769480 | tf_op jit(solution)/shard_map/cond/branch_0_fun/ppermute | solution.py:317
  121.4 28.3 %collective-permute-start.1 = (bf16[1152,256]{1,0:T(8,128)(2,1)S(1)}, bf16[1152,256]{1,0:T(8,128)(2,1)S(1)}, u32[]{:S(2)}, u32[]{:S(2)}) collective-permute-start(bf16[1152,256]{1,0:T(8,128)(2,1)S(1)} %get-tuple-element.182), channel_id=1, source_target_pairs={{0,128},{64,192},{128,0},{192,64},{1,129},{65,193},{129,1},{193,65... | collective-permute-start | bytes 1769480 | tf_op jit(solution)/shard_map/cond/branch_0_fun/ppermute | solution.py:317
  124.1 25.6 %collective-permute-start.2 = (bf16[1152,256]{1,0:T(8,128)(2,1)S(1)}, bf16[1152,256]{1,0:T(8,128)(2,1)S(1)}, u32[]{:S(2)}, u32[]{:S(2)}) collective-permute-start(bf16[1152,256]{1,0:T(8,128)(2,1)S(1)} %get-tuple-element.183), channel_id=1, source_target_pairs={{0,192},{64,0},{128,64},{192,128},{1,193},{65,1},{129,65},{193,129... | collective-permute-start | bytes 1769480 | tf_op jit(solution)/shard_map/cond/branch_0_fun/ppermute | solution.py:317
  126.5 12.2 %copy-start.10 = (bf16[224,512]{1,0:T(8,128)(2,1)S(1)}, bf16[224,512]{1,0:T(8,128)(2,1)}, u32[]{:S(2)}) copy-start(bf16[224,512]{1,0:T(8,128)(2,1)} %get-tuple-element.189.x_ref) | copy-start | bytes 688132 | tf_op jit(solution)/shard_map/cond
  139.2 5.6 %collective-permute-start.3 = (bf16[128,256]{1,0:T(8,128)(2,1)S(1)}, bf16[128,256]{1,0:T(8,128)(2,1)S(1)}, u32[]{:S(2)}, u32[]{:S(2)}) collective-permute-start(bf16[128,256]{1,0:T(8,128)(2,1)S(1)} %get-tuple-element.191), channel_id=1, source_target_pairs={{0,64},{64,128},{128,192},{192,0},{1,65},{65,129},{129,193},{193,1... | collective-permute-start | bytes 196616 | tf_op jit(solution)/shard_map/cond/branch_0_fun/ppermute | solution.py:317
  139.9 5.9 %collective-permute-start.4 = (bf16[128,256]{1,0:T(8,128)(2,1)S(1)}, bf16[128,256]{1,0:T(8,128)(2,1)S(1)}, u32[]{:S(2)}, u32[]{:S(2)}) collective-permute-start(bf16[128,256]{1,0:T(8,128)(2,1)S(1)} %get-tuple-element.192), channel_id=1, source_target_pairs={{0,128},{64,192},{128,0},{192,64},{1,129},{65,193},{129,1},{193,65... | collective-permute-start | bytes 196616 | tf_op jit(solution)/shard_map/cond/branch_0_fun/ppermute | solution.py:317
  144.8 4.3 %collective-permute-start.5 = (bf16[128,256]{1,0:T(8,128)(2,1)S(1)}, bf16[128,256]{1,0:T(8,128)(2,1)S(1)}, u32[]{:S(2)}, u32[]{:S(2)}) collective-permute-start(bf16[128,256]{1,0:T(8,128)(2,1)S(1)} %get-tuple-element.193), channel_id=1, source_target_pairs={{0,192},{64,0},{128,64},{192,128},{1,193},{65,1},{129,65},{193,129... | collective-permute-start | bytes 196616 | tf_op jit(solution)/shard_map/cond/branch_0_fun/ppermute | solution.py:317
